TPU v7x, 32 devices: a whole 2x2x4 slice. The times are simulated.
32 devices in a mesh: fsdp: 4 (over y, x), ctx: 2 (over core), tp: 4 (over z).
Axes of the slice: x: 2, y: 2, z: 4, core: 2. Of those that a mesh axis runs over, the one named last changes fastest.
Arguments:
- block_input: float32 [4, 1024, 2048], P('fsdp', 'ctx'), may hold values from -6 to 6
- cotangent: float32 [4, 1024, 2048], P('fsdp', 'ctx'), may hold values from -6 to 6
- w_query: bfloat16 [2048, 2048], P(('fsdp', 'ctx'), 'tp'), may hold values from -0.125 to 0.125
- w_key: bfloat16 [2048, 512], P(('fsdp', 'ctx'), 'tp'), may hold values from -0.125 to 0.125
- w_value: bfloat16 [2048, 512], P(('fsdp', 'ctx'), 'tp'), may hold values from -0.125 to 0.125
- w_output: bfloat16 [2048, 2048], P('tp', ('fsdp', 'ctx')), may hold values from -4 to 4
- w_gate: bfloat16 [2048, 8192], P(('fsdp', 'ctx'), 'tp'), may hold values from -0.125 to 0.125
- w_up: bfloat16 [2048, 8192], P(('fsdp', 'ctx'), 'tp'), may hold values from -0.125 to 0.125
- w_down: bfloat16 [8192, 2048], P('tp', ('fsdp', 'ctx')), may hold values from -0.0625 to 0.0625
- attn_gain: bfloat16 [2048], P(('fsdp', 'ctx')), may hold values from 0.5 to 1.5
- ffn_gain: bfloat16 [2048], P(('fsdp', 'ctx')), may hold values from 0.5 to 1.5
Outputs:
- block_output: float32 [4, 1024, 2048], P('fsdp', 'ctx')
- input_grad: float32 [4, 1024, 2048], P('fsdp', 'ctx')
- grad_query: float32 [2048, 2048], P(('fsdp', 'ctx'), 'tp')
- grad_key: float32 [2048, 512], P(('fsdp', 'ctx'), 'tp')
- grad_value: float32 [2048, 512], P(('fsdp', 'ctx'), 'tp')
- grad_output: float32 [2048, 2048], P('tp', ('fsdp', 'ctx'))
- grad_gate: float32 [2048, 8192], P(('fsdp', 'ctx'), 'tp')
- grad_up: float32 [2048, 8192], P(('fsdp', 'ctx'), 'tp')
- grad_down: float32 [8192, 2048], P('tp', ('fsdp', 'ctx'))
- grad_attn_gain: float32 [2048], P(('fsdp', 'ctx'))
- grad_ffn_gain: float32 [2048], P(('fsdp', 'ctx'))
All inputs are finite; a program needn't handle non-finite values.
Results may differ from a plain program's by a relative error of at most 0.013.
Values may be sent and summed in bfloat16 or wider, within the bound.
No kernel may reach another device: no remote copies, remote signals or barrier semaphores. Data moves between devices by JAX's collectives and lax.ppermute only.
A program may use at most 256 MiB of HBM per device.

v0:
```python
import jax
import jax.numpy as jnp
from jax import lax
from jax.sharding import PartitionSpec as P

HD = 64
EPS = 1e-05
BASE = 500000.0
NEG = -1e30


def shifted(shard, axis, by):
    count = lax.axis_size(axis)
    pairs = [(i, i + by) for i in range(count) if 0 <= i + by < count]
    return lax.ppermute(shard, axis, pairs)


def rotate(values, positions, sign):
    half = values.shape[-1] // 2
    inverse = BASE ** (-(jnp.arange(half, dtype=jnp.float32) * 2.0) / values.shape[-1])
    angle = positions.astype(jnp.float32)[:, None] * inverse[None, :]
    cosine = jnp.cos(angle)[:, None, :]
    sine = sign * jnp.sin(angle)[:, None, :]
    first = values[..., :half]
    second = values[..., half:]
    return jnp.concatenate(
        [first * cosine - second * sine, second * cosine + first * sine], axis=-1
    )


def norm_forward(rows, gain):
    scale = lax.rsqrt(jnp.mean(rows * rows, axis=-1, keepdims=True) + EPS)
    return (rows * scale * gain, scale)


def norm_backward(rows, scale, gain, grad):
    weighted = grad * gain
    d_rows = scale * weighted - rows * scale**3 * jnp.mean(weighted * rows, axis=-1, keepdims=True)
    return (d_rows, jnp.sum(grad * rows * scale, axis=0))


def forward_block(queries, keys, vals, allow, scale):
    scores = jnp.einsum("gbd,kd->gbk", queries, keys, preferred_element_type=jnp.float32) * scale
    scores = jnp.where(allow[None], scores, NEG)
    top = jnp.max(scores, axis=-1, keepdims=True)
    total = top[..., 0] + jnp.log(jnp.sum(jnp.exp(scores - top), axis=-1))
    probs = jnp.exp(scores - total[..., None]).astype(jnp.bfloat16)
    out = jnp.einsum("gbk,kd->gbd", probs, vals, preferred_element_type=jnp.float32)
    return (out.astype(jnp.bfloat16), total)


def backward_block(queries, keys, vals, allow, total, grad_out, out, scale):
    scores = jnp.einsum("gbd,kd->gbk", queries, keys, preferred_element_type=jnp.float32) * scale
    scores = jnp.where(allow[None], scores, NEG)
    probs = jnp.exp(scores - total[..., None])
    rounded = probs.astype(jnp.bfloat16)
    d_vals = jnp.einsum("gbk,gbd->kd", rounded, grad_out, preferred_element_type=jnp.float32)
    d_probs = jnp.einsum("gbd,kd->gbk", grad_out, vals, preferred_element_type=jnp.float32)
    delta = jnp.sum(grad_out.astype(jnp.float32) * out.astype(jnp.float32), axis=-1)
    d_scores = (probs * (d_probs - delta[..., None]) * scale).astype(jnp.bfloat16)
    d_query = jnp.einsum("gbk,kd->gbd", d_scores, keys, preferred_element_type=jnp.float32)
    d_keys = jnp.einsum("gbk,gbd->kd", d_scores, queries, preferred_element_type=jnp.float32)
    return (d_query, d_keys, d_vals)


def split_blocks(tensor, count, block):
    return tensor.reshape((tensor.shape[0], count, block) + tensor.shape[2:]).swapaxes(0, 1)


def attention_forward(grouped, keys, vals, allow, block, scale):

    def per_head(items):
        head_q, head_k, head_v = items
        groups, rows, width = head_q.shape
        count = rows // block
        outs, totals = lax.map(
            lambda piece: forward_block(piece[0], head_k, head_v, piece[1], scale),
            (split_blocks(head_q, count, block), allow.reshape(count, block, allow.shape[1])),
        )
        return (
            outs.swapaxes(0, 1).reshape(groups, rows, width),
            totals.swapaxes(0, 1).reshape(groups, rows),
        )

    return lax.map(per_head, (grouped, keys, vals))


def attention_backward(grouped, keys, vals, allow, totals, grads, outs, block, scale):

    def per_head(items):
        head_q, head_k, head_v, head_t, head_g, head_o = items
        groups, rows, width = head_q.shape
        count = rows // block

        def step(carry, piece):
            d_query, d_keys, d_vals = backward_block(
                piece[0], head_k, head_v, piece[1], piece[2], piece[3], piece[4], scale
            )
            return ((carry[0] + d_keys, carry[1] + d_vals), d_query)

        zeros = jnp.zeros(head_k.shape, jnp.float32)
        pieces = (
            split_blocks(head_q, count, block),
            allow.reshape(count, block, allow.shape[1]),
            split_blocks(head_t, count, block),
            split_blocks(head_g, count, block),
            split_blocks(head_o, count, block),
        )
        (d_keys, d_vals), d_query = lax.scan(step, (zeros, zeros), pieces)
        return (d_query.swapaxes(0, 1).reshape(groups, rows, width), d_keys, d_vals)

    return lax.map(per_head, (grouped, keys, vals, totals, grads, outs))


def dotf(left, right):
    return jnp.dot(left, right, preferred_element_type=jnp.float32)


def body(
    block_input,
    cotangent,
    w_query,
    w_key,
    w_value,
    w_output,
    w_gate,
    w_up,
    w_down,
    attn_gain,
    ffn_gain,
):
    wq, wk, wv, wo, wg, wu, wd, gain_qa, gain_qf = (
        lax.all_gather(w_query, ("fsdp", "ctx"), axis=0, tiled=True),
        lax.all_gather(w_key, ("fsdp", "ctx"), axis=0, tiled=True),
        lax.all_gather(w_value, ("fsdp", "ctx"), axis=0, tiled=True),
        lax.all_gather(w_output, ("fsdp", "ctx"), axis=1, tiled=True),
        lax.all_gather(w_gate, ("fsdp", "ctx"), axis=0, tiled=True),
        lax.all_gather(w_up, ("fsdp", "ctx"), axis=0, tiled=True),
        lax.all_gather(w_down, ("fsdp", "ctx"), axis=1, tiled=True),
        lax.all_gather(attn_gain, ("fsdp", "ctx"), axis=0, tiled=True),
        lax.all_gather(ffn_gain, ("fsdp", "ctx"), axis=0, tiled=True),
    )
    rows = block_input[0]
    cot = cotangent[0]
    local = rows.shape[0]
    block = min(512, local)
    scale = HD ** (-0.5)
    heads = wq.shape[1] // HD
    kv_heads = wk.shape[1] // HD
    groups = heads // kv_heads
    place = lax.axis_index("ctx")
    positions = place * local + jnp.arange(local, dtype=jnp.int32)
    gain_a = gain_qa.astype(jnp.float32)
    gain_f = gain_qf.astype(jnp.float32)
    normed_f, scale_a = norm_forward(rows, gain_a)
    normed = normed_f.astype(jnp.bfloat16)
    query = dotf(normed, wq).reshape(local, heads, HD)
    keys = dotf(normed, wk).reshape(local, kv_heads, HD)
    vals = dotf(normed, wv)
    query_rot = rotate(query, positions, 1.0).astype(jnp.bfloat16)
    keys_rot = rotate(keys, positions, 1.0).astype(jnp.bfloat16).reshape(local, kv_heads * HD)
    vals_b = vals.astype(jnp.bfloat16)
    keys_prev, vals_prev = shifted((keys_rot, vals_b), "ctx", 1)
    all_keys = (
        jnp.concatenate([keys_prev, keys_rot], axis=0)
        .reshape(2 * local, kv_heads, HD)
        .transpose(1, 0, 2)
    )
    all_vals = (
        jnp.concatenate([vals_prev, vals_b], axis=0)
        .reshape(2 * local, kv_heads, HD)
        .transpose(1, 0, 2)
    )
    grouped = query_rot.reshape(local, kv_heads, groups, HD).transpose(1, 2, 0, 3)
    index = jnp.arange(local, dtype=jnp.int32)
    earlier = jnp.broadcast_to(place > 0, (local, local))
    causal = index[None, :] <= index[:, None]
    allow = jnp.concatenate([earlier, causal], axis=1)
    attn, totals = attention_forward(grouped, all_keys, all_vals, allow, block, scale)
    attn_flat = attn.transpose(2, 0, 1, 3).reshape(local, heads * HD)
    hidden = rows + lax.psum(dotf(attn_flat, wo), "tp")
    hnorm_f, scale_f = norm_forward(hidden, gain_f)
    hnorm = hnorm_f.astype(jnp.bfloat16)
    gate = dotf(hnorm, wg)
    up = dotf(hnorm, wu)
    sigma = jax.nn.sigmoid(gate)
    active = gate * sigma
    inner = (active * up).astype(jnp.bfloat16)
    out = hidden + lax.psum(dotf(inner, wd).astype(jnp.bfloat16), "tp").astype(jnp.float32)
    cot_b = cot.astype(jnp.bfloat16)
    d_inner = dotf(cot_b, wd.T)
    d_gate = (d_inner * up * sigma * (1.0 + gate * (1.0 - sigma))).astype(jnp.bfloat16)
    d_up = (d_inner * active).astype(jnp.bfloat16)
    d_hnorm = lax.psum(dotf(d_gate, wg.T) + dotf(d_up, wu.T), "tp")
    d_norm, g_ffn = norm_backward(hidden, scale_f, gain_f, d_hnorm)
    d_hidden = cot + d_norm
    dh_b = d_hidden.astype(jnp.bfloat16)
    d_attn = (
        dotf(dh_b, wo.T)
        .astype(jnp.bfloat16)
        .reshape(local, kv_heads, groups, HD)
        .transpose(1, 2, 0, 3)
    )
    d_query, d_keys, d_vals = attention_backward(
        grouped, all_keys, all_vals, allow, totals, d_attn, attn, block, scale
    )
    keys_grad = d_keys.transpose(1, 0, 2).reshape(2 * local, kv_heads * HD)
    vals_grad = d_vals.transpose(1, 0, 2).reshape(2 * local, kv_heads * HD)
    keys_back, vals_back = shifted((keys_grad[:local], vals_grad[:local]), "ctx", -1)
    keys_own = keys_grad[local:] + keys_back
    vals_own = vals_grad[local:] + vals_back
    d_query = d_query.transpose(2, 0, 1, 3).reshape(local, heads, HD)
    dq_b = rotate(d_query, positions, -1.0).astype(jnp.bfloat16).reshape(local, heads * HD)
    dk_b = (
        rotate(keys_own.reshape(local, kv_heads, HD), positions, -1.0)
        .astype(jnp.bfloat16)
        .reshape(local, kv_heads * HD)
    )
    dv_b = vals_own.astype(jnp.bfloat16)
    d_normed = lax.psum(dotf(dq_b, wq.T) + dotf(dk_b, wk.T) + dotf(dv_b, wv.T), "tp")
    d_rows, g_attn = norm_backward(rows, scale_a, gain_a, d_normed)
    d_input = d_hidden + d_rows
    s_query, s_key, s_value, s_output, s_gate, s_up, s_down, s_attn, s_ffn = (
        lax.psum_scatter(dotf(normed.T, dq_b), ("fsdp", "ctx"), scatter_dimension=0, tiled=True),
        lax.psum_scatter(dotf(normed.T, dk_b), ("fsdp", "ctx"), scatter_dimension=0, tiled=True),
        lax.psum_scatter(dotf(normed.T, dv_b), ("fsdp", "ctx"), scatter_dimension=0, tiled=True),
        lax.psum_scatter(dotf(attn_flat.T, dh_b), ("fsdp", "ctx"), scatter_dimension=1, tiled=True),
        lax.psum_scatter(dotf(hnorm.T, d_gate), ("fsdp", "ctx"), scatter_dimension=0, tiled=True),
        lax.psum_scatter(dotf(hnorm.T, d_up), ("fsdp", "ctx"), scatter_dimension=0, tiled=True),
        lax.psum_scatter(dotf(inner.T, cot_b), ("fsdp", "ctx"), scatter_dimension=1, tiled=True),
        lax.psum_scatter(g_attn, ("fsdp", "ctx"), scatter_dimension=0, tiled=True),
        lax.psum_scatter(g_ffn, ("fsdp", "ctx"), scatter_dimension=0, tiled=True),
    )
    return (
        out[None],
        d_input[None],
        s_query,
        s_key,
        s_value,
        s_output,
        s_gate,
        s_up,
        s_down,
        s_attn,
        s_ffn,
    )


def solution(mesh):
    placed = (
        P("fsdp", "ctx", None),
        P("fsdp", "ctx", None),
        P(("fsdp", "ctx"), "tp"),
        P(("fsdp", "ctx"), "tp"),
        P(("fsdp", "ctx"), "tp"),
        P("tp", ("fsdp", "ctx")),
        P(("fsdp", "ctx"), "tp"),
        P(("fsdp", "ctx"), "tp"),
        P("tp", ("fsdp", "ctx")),
        P(("fsdp", "ctx")),
        P(("fsdp", "ctx")),
    )
    return jax.shard_map(
        body,
        mesh=mesh,
        in_specs=placed,
        out_specs=(
            P("fsdp", "ctx", None),
            P("fsdp", "ctx", None),
            P(("fsdp", "ctx"), "tp"),
            P(("fsdp", "ctx"), "tp"),
            P(("fsdp", "ctx"), "tp"),
            P("tp", ("fsdp", "ctx")),
            P(("fsdp", "ctx"), "tp"),
            P(("fsdp", "ctx"), "tp"),
            P("tp", ("fsdp", "ctx")),
            P(("fsdp", "ctx")),
            P(("fsdp", "ctx")),
        ),
        check_vma=False,
    )
```

profile of v0, /device:TPU:0, one launch (start us, length us, event | category | flops | bytes accessed | tf_op | source)
XLA Modules:
  0.0 1437.5 jit_solution(5688634115593749319)
XLA Ops:
  8.6 10.4 all-gather
  19.0 10.7 all_gather.29
  30.0 3.0 fusion.52
  36.5 2.9 collective-permute-start
  39.4 8.9 all_gather.30
  51.5 2.9 collective-permute-start.1
  59.2 3.9 copy.28
  63.2 2.9 fusion.65
  66.3 12.7 while.10
  79.0 4.0 all-gather.10.cloned.1.call-done
  83.0 4.9 fusion.86
  89.7 9.1 all-gather.1
  98.8 144.2 %all-reduce.9.cloned.1.call-done = f32[512,2048]{1,0:T(8,128)} async-done(((f32[512,2048]{1,0:T(8,128)}), f32[512,2048]{1,0:T(8,128)}) %all-reduce.9.cloned.1.call-update) | async-done | bytes 4194320 | tf_op jit(solution)/shard_map/psum | solution.py:181
  243.0 4.0 multiply_reduce_fusion.2
  250.8 47.2 %all-gather.12.cloned.1.call-done = bf16[2048,2048]{1,0:T(8,128)(2,1)} async-done(((bf16[256,2048]{1,0:T(8,128)(2,1)}), bf16[2048,2048]{1,0:T(8,128)(2,1)}) %all-gather.12.cloned.1.call-update) | async-done | bytes 8388624 | tf_op jit(solution)/shard_map/all_gather | solution.py:137
  298.0 10.5 fusion.87
  308.6 45.5 %all-gather.14.cloned.1.call-done = bf16[2048,2048]{1,0:T(8,128)(2,1)} async-done(((bf16[256,2048]{1,0:T(8,128)(2,1)}), bf16[2048,2048]{1,0:T(8,128)(2,1)}) %all-gather.14.cloned.1.call-update) | async-done | bytes 8388624 | tf_op jit(solution)/shard_map/all_gather | solution.py:138
  354.1 10.5 fusion.88
  364.6 47.1 %all-gather.16.cloned.1.call-done = bf16[2048,2048]{1,0:T(8,128)(2,1)} async-done(((bf16[2048,256]{1,0:T(8,128)(2,1)}), bf16[2048,2048]{1,0:T(8,128)(2,1)}) %all-gather.16.cloned.1.call-update) | async-done | bytes 8388624 | tf_op jit(solution)/shard_map/all_gather | solution.py:139
  411.7 15.3 %multiply_convert_fusion.1 = (bf16[512,2048]{1,0:T(8,128)(2,1)S(1)}, bf16[512,2048]{1,0:T(8,128)(2,1)}, bf16[512,2048]{1,0:T(8,128)(2,1)}) fusion(f32[512,2048]{1,0:T(8,128)} %fusion.87, f32[512,2048]{1,0:T(8,128)} %fusion.88, bf16[2048,2048]{1,0:T(8,128)(2,1)} %all-gather.16.cloned.1.call-done, f32[1,512,2048]{2,1,0:T(8,128)} %param.16), kind=kOutput, calls=%fused_computation.79 | convolution fusion | flops 4310695936 | bytes 27262976 | tf_op jit(solution)/shard_map/dot_general | solution.py:116
  427.0 8.4 fusion.89
  435.4 6.1 convolution_add_fusion
  441.6 9.8 convolution_convert_fusion
  451.7 145.0 %all-reduce.13.cloned.1.call-done = f32[512,2048]{1,0:T(8,128)} async-done(((f32[512,2048]{1,0:T(8,128)}), f32[512,2048]{1,0:T(8,128)}) %all-reduce.13.cloned.1.call-update) | async-done | bytes 4194320 | tf_op jit(solution)/shard_map/psum | solution.py:194
  596.7 4.5 multiply_reduce_fusion
  601.2 83.0 %all-reduce.11.cloned.1.call-done = bf16[512,2048]{1,0:T(8,128)(2,1)} async-done(((bf16[512,2048]{1,0:T(8,128)(2,1)}), bf16[512,2048]{1,0:T(8,128)(2,1)}) %all-reduce.11.cloned.1.call-update) | async-done | bytes 2097168 | tf_op jit(solution)/shard_map/psum | solution.py:189
  684.2 8.1 bitcast_add_fusion
  695.6 20.4 %while.27 = (s32[]{:T(128)}, f32[2,4,512,64]{2,3,1,0:T(8,128)}, f32[2,1024,64]{1,2,0:T(8,128)S(1)}, f32[2,1024,64]{1,2,0:T(8,128)}, pred[512,1024]{1,0:T(8,128)(...) while((s32[]{:T(128)}, f32[2,4,512,64]{2,3,1,0:T(8,128)}, ...), condition=%wide.region_12.13_spmd, body=%wide.region_10.12_spmd.sunk | while | flops 1365768192 | bytes 50255028 | solution.py:112
  697.1 3.3 multiply_convert_fusion.7
  702.8 3.1 fusion.170
  707.3 3.3 multiply_convert_fusion.7
  713.0 3.1 fusion.170
  726.8 3.5 fusion.92
  732.2 5.7 fusion.73
  738.0 3.3 fusion.69
  742.9 9.7 fusion.93
  752.7 9.9 fusion.94
  764.1 10.4 fusion.82
  776.4 105.3 %all-reduce.15.cloned.1.call-done = f32[512,2048]{1,0:T(8,128)} async-done(((f32[512,2048]{1,0:T(8,128)}), f32[512,2048]{1,0:T(8,128)}) %all-reduce.15.cloned.1.call-update) | async-done | bytes 4194320 | tf_op jit(solution)/shard_map/psum | solution.py:220
  881.7 4.5 fusion.61
  886.2 24.1 %all-reduce.3 = (f32[2048]{0:T(1024)S(1)}, f32[2048]{0:T(1024)S(1)}) all-reduce(f32[2048]{0:T(1024)S(1)} %get-tuple-element.169, f32[2048]{0:T(1024)S(1)} %get-tuple-element.167), channel_id=9, replica_groups=mesh['fsdp'=4,'ctx'=2,'tp'=4] {'fsdp','ctx'}, use_global_device_ids=true, to_apply=%region_23.24.clone | all-reduce | flops 4096 | bytes 32768
  911.6 7.8 fusion.58
  920.3 39.8 %reduce-scatter.10.cloned.1.call-done = f32[256,128]{1,0:T(8,128)} async-done(((f32[2048,128]{1,0:T(8,128)}), f32[256,128]{1,0:T(8,128)}) %reduce-scatter.10.cloned.1.call-update) | async-done | bytes 131088 | tf_op jit(solution)/shard_map/reduce_scatter | solution.py:225
  960.1 54.9 %reduce-scatter.14.cloned.1.call-done = f32[512,256]{1,0:T(8,128)} async-done(((f32[512,2048]{1,0:T(8,128)}), f32[512,256]{1,0:T(8,128)}) %reduce-scatter.14.cloned.1.call-update) | async-done | bytes 524304 | tf_op jit(solution)/shard_map/reduce_scatter | solution.py:227
  1015.0 55.1 %reduce-scatter.8.cloned.1.call-done = f32[256,512]{1,0:T(8,128)} async-done(((f32[2048,512]{1,0:T(8,128)}), f32[256,512]{1,0:T(8,128)}) %reduce-scatter.8.cloned.1.call-update) | async-done | bytes 524304 | tf_op jit(solution)/shard_map/reduce_scatter | solution.py:224
  1070.1 120.2 %reduce-scatter.16.cloned.1.call-done = f32[256,2048]{1,0:T(8,128)} async-done(((f32[2048,2048]{1,0:T(8,128)}), f32[256,2048]{1,0:T(8,128)}) %reduce-scatter.16.cloned.1.call-update) | async-done | bytes 2097168 | tf_op jit(solution)/shard_map/reduce_scatter | solution.py:228
  1190.3 120.2 %reduce-scatter.18.cloned.1.call-done = f32[256,2048]{1,0:T(8,128)} async-done(((f32[2048,2048]{1,0:T(8,128)}), f32[256,2048]{1,0:T(8,128)}) %reduce-scatter.18.cloned.1.call-update) | async-done | bytes 2097168 | tf_op jit(solution)/shard_map/reduce_scatter | solution.py:229
  1310.5 120.0 %reduce-scatter.20.cloned.1.call-done = f32[2048,256]{1,0:T(8,128)} async-done(((f32[2048,2048]{1,0:T(8,128)}), f32[2048,256]{1,0:T(8,128)}) %reduce-scatter.20.cloned.1.call-update) | async-done | bytes 2097168 | tf_op jit(solution)/shard_map/reduce_scatter | solution.py:230
  (173 shorter events, 61.7 us)
Async XLA Ops:
  7.2 52.1 %all-gather.8.cloned.1.call-start = ((), (), s32[]{:S(2)}) async-start(), calls=%async_computation.7 | async-start | bytes 2359296 | tf_op jit(solution)/shard_map/all_gather | solution.py:133
  7.9 75.1 %all-gather.10.cloned.1.call-start = ((), (), s32[]{:S(2)}) async-start(), calls=%async_computation.8 | async-start | bytes 2359296 | tf_op jit(solution)/shard_map/all_gather | solution.py:136
  19.0 29.3 %copy-start.20 = (f32[8,1,256]{2,1,0:T(1,128)}, f32[8,1,256]{2,1,0:T(1,128)S(1)}, u32[]{:S(2)}) copy-start(f32[8,1,256]{2,1,0:T(1,128)S(1)} %convert_element_type.149) | copy-start | bytes 24580
  29.7 4.8 copy-start.7
  29.9 4.6 copy-start
  33.5 14.8 %copy-start.23 = (f32[512]{0:T(512)}, f32[512]{0:T(512)S(1)}, u32[]{:S(2)}) copy-start(f32[512]{0:T(512)S(1)} %get-tuple-element.236) | copy-start | bytes 6148
  34.5 31.6 %copy-start.13 = (f32[512,32]{0,1:T(8,128)}, f32[512,32]{0,1:T(8,128)S(1)}, u32[]{:S(2)}) copy-start(f32[512,32]{0,1:T(8,128)S(1)} %get-tuple-element.234) | copy-start | bytes 196612
  34.5 4.9 copy-start.22
  34.9 28.2 %copy-start.2 = (bf16[1,512,2048]{2,1,0:T(8,128)(2,1)}, bf16[1,512,2048]{2,1,0:T(8,128)(2,1)S(1)}, u32[]{:S(2)}) copy-start(bf16[1,512,2048]{2,1,0:T(8,128)(2,1)S(1)} %multiply_convert_fusion.5) | copy-start | bytes 6291460
  36.5 18.2 %collective-permute-start = (bf16[512,128]{0,1:T(8,128)(2,1)}, bf16[512,128]{0,1:T(8,128)(2,1)}, u32[]{:S(2)}, u32[]{:S(2)}) collective-permute-start(bf16[512,128]{0,1:T(8,128)(2,1)} %bitcast.31), channel_id=1, source_target_pairs={{0,4},{1,5},{2,6},{3,7},{8,12},{9,13},{10,14},{11,15},{16,20},{17,... | collective-permute-start | bytes 393224 | tf_op jit(solution)/shard_map/ppermute | solution.py:15
  48.3 3.2 copy-start.9
  51.5 4.2 collective-permute-start.1
  54.5 188.6 %all-reduce.9.cloned.1.call-start = ((), (), s32[]{:S(2)}) async-start(), calls=%async_computation.9 | async-start | bytes 8388608 | tf_op jit(solution)/shard_map/psum | solution.py:181
  67.9 2.4 copy-start.18
  74.3 2.4 copy-start.18
  87.9 1.8 copy-start.27
  87.9 210.1 %all-gather.12.cloned.1.call-start = ((), (), s32[]{:S(2)}) async-start(), calls=%async_computation.10 | async-start | bytes 9437184 | tf_op jit(solution)/shard_map/all_gather | solution.py:137
  88.5 265.6 %all-gather.14.cloned.1.call-start = ((), (), s32[]{:S(2)}) async-start(), calls=%async_computation.11 | async-start | bytes 9437184 | tf_op jit(solution)/shard_map/all_gather | solution.py:138
  89.1 322.6 %all-gather.16.cloned.1.call-start = ((), (), s32[]{:S(2)}) async-start(), calls=%async_computation.12 | async-start | bytes 9437184 | tf_op jit(solution)/shard_map/all_gather | solution.py:139
  89.7 507.0 %all-reduce.13.cloned.1.call-start = ((), (), s32[]{:S(2)}) async-start(), calls=%async_computation.14 | async-start | bytes 8388608 | tf_op jit(solution)/shard_map/psum | solution.py:194
  247.0 2.0 copy-start.1
  426.9 8.4 copy-start.30
  426.9 8.4 copy-start.26
  441.6 242.6 %all-reduce.11.cloned.1.call-start = ((), (), s32[]{:S(2)}) async-start(), calls=%async_computation.13 | async-start | bytes 4194304 | tf_op jit(solution)/shard_map/psum | solution.py:189
  451.4 430.3 %all-reduce.15.cloned.1.call-start = ((), (), s32[]{:S(2)}) async-start(), calls=%async_computation.15 | async-start | bytes 8388608 | tf_op jit(solution)/shard_map/psum | solution.py:220
  684.2 10.1 copy-start.12
  692.3 2.0 copy-start.4
  692.3 3.3 copy-start.19
  695.6 24.5 %copy-start.14 = (f32[512,32]{0,1:T(8,128)S(1)}, f32[512,32]{0,1:T(8,128)}, u32[]{:S(2)}) copy-start(f32[512,32]{0,1:T(8,128)} %copy-done.13) | copy-start | bytes 196612
  695.6 24.5 %copy-start.17 = (f32[512,32]{0,1:T(8,128)S(1)}, f32[512,32]{0,1:T(8,128)}, u32[]{:S(2)}) copy-start(f32[512,32]{0,1:T(8,128)} %get-tuple-element.232) | copy-start | bytes 196612
  697.0 3.3 copy-start.15
  707.3 3.3 copy-start.15
  716.1 5.5 copy-start.6
  717.3 6.5 collective-permute-start.3
  718.6 4.3 collective-permute-start.2
  726.8 3.6 copy-start.3
  726.8 193.6 %reduce-scatter.12.cloned.1.call-start = ((), (), s32[]{:S(2)}) async-start(), calls=%async_computation.18 | async-start | bytes 1179648 | tf_op jit(solution)/shard_map/reduce_scatter | solution.py:226
  730.3 229.8 %reduce-scatter.10.cloned.1.call-start = ((), (), s32[]{:S(2)}) async-start(), calls=%async_computation.17 | async-start | bytes 1179648 | tf_op jit(solution)/shard_map/reduce_scatter | solution.py:225
  732.2 282.8 %reduce-scatter.14.cloned.1.call-start = ((), (), s32[]{:S(2)}) async-start(), calls=%async_computation.19 | async-start | bytes 4718592 | tf_op jit(solution)/shard_map/reduce_scatter | solution.py:227
  737.9 332.2 %reduce-scatter.8.cloned.1.call-start = ((), (), s32[]{:S(2)}) async-start(), calls=%async_computation.16 | async-start | bytes 4718592 | tf_op jit(solution)/shard_map/reduce_scatter | solution.py:224
  741.3 1.6 copy-start.11
  741.3 449.0 %reduce-scatter.16.cloned.1.call-start = ((), (), s32[]{:S(2)}) async-start(), calls=%async_computation.20 | async-start | bytes 18874368 | tf_op jit(solution)/shard_map/reduce_scatter | solution.py:228
  752.6 557.9 %reduce-scatter.18.cloned.1.call-start = ((), (), s32[]{:S(2)}) async-start(), calls=%async_computation.21 | async-start | bytes 18874368 | tf_op jit(solution)/shard_map/reduce_scatter | solution.py:229
  762.6 1.6 copy-start.29
  762.6 668.0 %reduce-scatter.20.cloned.1.call-start = ((), (), s32[]{:S(2)}) async-start(), calls=%async_computation.22 | async-start | bytes 18874368 | tf_op jit(solution)/shard_map/reduce_scatter | solution.py:230
  774.5 107.2 %copy-start.21 = (f32[8,1,256]{2,1,0:T(1,128)S(1)}, f32[8,1,256]{2,1,0:T(1,128)}, u32[]{:S(2)}) copy-start(f32[8,1,256]{2,1,0:T(1,128)} %copy-done.20) | copy-start | bytes 24580
  774.6 107.2 %copy-start.24 = (f32[512]{0:T(512)S(1)}, f32[512]{0:T(512)}, u32[]{:S(2)}) copy-start(f32[512]{0:T(512)} %copy-done.23) | copy-start | bytes 6148
  776.4 135.1 %copy-start.25 = (f32[512]{0:T(512)S(1)}, f32[512]{0:T(512)}, u32[]{:S(2)}) copy-start(f32[512]{0:T(512)} %get-tuple-element.235) | copy-start | bytes 6148
  (6 other events, 6.5 us)
Sparse Core Ops, SparseCore 0:
  9.9 31.1 all-gather.7
  54.6 28.3 all-gather.9
  88.0 154.9 all-reduce.8
  244.8 53.2 all-gather.11
  299.8 54.2 all-gather.13
  355.8 55.8 all-gather.15
  441.7 154.9 all-reduce.12
  599.0 85.0 all-reduce.10
  726.9 154.7 all-reduce.14
  885.3 34.9 reduce-scatter.11
  924.1 35.9 reduce-scatter.9
  963.9 51.0 reduce-scatter.13
  1018.9 51.1 reduce-scatter.7
  1074.1 116.1 reduce-scatter.15
  1194.3 116.1 reduce-scatter.17
  1314.5 115.9 reduce-scatter.19
where the time goes:
time: 1450 us; the launch traced here: 1440 us
  waiting for transfers between devices  1130 us (78%)
  matrix products  149 us (10%)
  blocking collectives  63.1 us (4%)
  other arithmetic  46.2 us (3%)
  local copies, waits for them, and re-layouts  19 us (1%)
  between operations  15.6 us (1%)
    psum x1, waiting for transfers between devices, body(): d_hnorm = lax.psum(dotf(d_gate, wg.T) + dotf(d_up, wu.T), 'tp')  145 us
    psum x1, waiting for transfers between devices, body(): hidden = rows + lax.psum(dotf(attn_flat, wo), 'tp')  144 us
    dot_general x21, matrix products, dotf(): return jnp.dot(left, right, preferred_element_type=jnp.float32)  121 us
    reduce_scatter x1, waiting for transfers between devices, body(): lax.psum_scatter(dotf(hnorm.T, d_gate), ('fsdp', 'ctx'), scatter_dimensio...  120 us
    reduce_scatter x1, waiting for transfers between devices, body(): lax.psum_scatter(dotf(hnorm.T, d_up), ('fsdp', 'ctx'), scatter_dimension=...  120 us
    reduce_scatter x1, waiting for transfers between devices, body(): lax.psum_scatter(dotf(inner.T, cot_b), ('fsdp', 'ctx'), scatter_dimension...  120 us
    psum x1, waiting for transfers between devices, body(): lax.psum(dotf(dq_b, wq.T) + dotf(dk_b, wk.T) + dotf(dv_b, wv.T), 'tp')  105 us
    psum x1, waiting for transfers between devices, body(): lax.psum(dotf(inner, wd).astype(jnp.bfloat16), 'tp').astype(jnp.float32)  83 us
  transfers between devices with their start and end apart: 20, of which 15 were waited for; matrix products, arithmetic and copies ran while one was open for 9% of the time, Pallas kernels for 0%

commit v1 on v0

--- a/solution.py
+++ b/solution.py
@@ -178,7 +178,7 @@
     allow = jnp.concatenate([earlier, causal], axis=1)
     attn, totals = attention_forward(grouped, all_keys, all_vals, allow, block, scale)
     attn_flat = attn.transpose(2, 0, 1, 3).reshape(local, heads * HD)
-    hidden = rows + lax.psum(dotf(attn_flat, wo), "tp")
+    hidden = rows + jnp.sum(lax.all_gather(dotf(attn_flat, wo), "tp"), axis=0)
     hnorm_f, scale_f = norm_forward(hidden, gain_f)
     hnorm = hnorm_f.astype(jnp.bfloat16)
     gate = dotf(hnorm, wg)

time: 1450 us -> 1580 us (1.090)
  waiting for transfers between devices: 1130 us -> 1260 us
    all_gather x0 -> x1, waiting for transfers between devices: none -> 276 us  [body(): hidden = rows + jnp.sum(lax.all_gather(dotf(attn_flat, wo), 'tp'), axis=0)]
    psum x1 -> x0, waiting for transfers between devices: 144 us -> none  [body(): hidden = rows + lax.psum(dotf(attn_flat, wo), 'tp')]
where the time goes in v1:
time: 1580 us; the launch traced here: 1570 us
  waiting for transfers between devices  1260 us (80%)
  matrix products  149 us (9%)
  blocking collectives  63.1 us (4%)
  other arithmetic  56.4 us (4%)
  local copies, waits for them, and re-layouts  19.1 us (1%)
    all_gather x1, waiting for transfers between devices, body(): hidden = rows + jnp.sum(lax.all_gather(dotf(attn_flat, wo), 'tp'), axis=0)  276 us
    psum x1, waiting for transfers between devices, body(): d_hnorm = lax.psum(dotf(d_gate, wg.T) + dotf(d_up, wu.T), 'tp')  145 us
    dot_general x21, matrix products, dotf(): return jnp.dot(left, right, preferred_element_type=jnp.float32)  121 us
    reduce_scatter x1, waiting for transfers between devices, body(): lax.psum_scatter(dotf(hnorm.T, d_gate), ('fsdp', 'ctx'), scatter_dimensio...  120 us
    reduce_scatter x1, waiting for transfers between devices, body(): lax.psum_scatter(dotf(hnorm.T, d_up), ('fsdp', 'ctx'), scatter_dimension=...  120 us
    reduce_scatter x1, waiting for transfers between devices, body(): lax.psum_scatter(dotf(inner.T, cot_b), ('fsdp', 'ctx'), scatter_dimension...  120 us
    psum x1, waiting for transfers between devices, body(): lax.psum(dotf(dq_b, wq.T) + dotf(dk_b, wk.T) + dotf(dv_b, wv.T), 'tp')  105 us
    psum x1, waiting for transfers between devices, body(): lax.psum(dotf(inner, wd).astype(jnp.bfloat16), 'tp').astype(jnp.float32)  83 us
  transfers between devices with their start and end apart: 20, of which 15 were waited for; matrix products, arithmetic and copies ran while one was open for 9% of the time, Pallas kernels for 0%

profile of v1, /device:TPU:0, one launch (start us, length us, event | category | flops | bytes accessed | tf_op | source)
XLA Modules:
  0.0 1568.5 jit_solution(9176219962569247049)
XLA Ops:
  8.6 10.4 all-gather.1
  19.0 10.7 all_gather.35
  30.0 3.0 fusion.52
  36.5 2.9 collective-permute-start
  39.4 8.9 all_gather.36
  51.5 2.9 collective-permute-start.1
  59.2 3.9 copy.28
  66.2 12.7 while.10
  78.9 4.0 all-gather.12.cloned.1.call-done
  83.0 4.9 fusion.86
  89.7 9.1 all-gather.2
  98.8 276.0 %all-gather.20.cloned.1.call-done = f32[2048,2048]{1,0:T(8,128)} async-done(((f32[512,2048]{1,0:T(8,128)}), f32[2048,2048]{1,0:T(8,128)}) %all-gather.20.cloned.1.call-update) | async-done | bytes 16777232 | tf_op jit(solution)/shard_map/all_gather | solution.py:181
  374.8 10.2 reduce_sum.84
  385.0 4.0 multiply_reduce_fusion.2
  392.7 36.3 %all-gather.14.cloned.1.call-done = bf16[2048,2048]{1,0:T(8,128)(2,1)} async-done(((bf16[256,2048]{1,0:T(8,128)(2,1)}), bf16[2048,2048]{1,0:T(8,128)(2,1)}) %all-gather.14.cloned.1.call-update) | async-done | bytes 8388624 | tf_op jit(solution)/shard_map/all_gather | solution.py:137
  429.0 10.5 fusion.87
  439.5 45.5 %all-gather.16.cloned.1.call-done = bf16[2048,2048]{1,0:T(8,128)(2,1)} async-done(((bf16[256,2048]{1,0:T(8,128)(2,1)}), bf16[2048,2048]{1,0:T(8,128)(2,1)}) %all-gather.16.cloned.1.call-update) | async-done | bytes 8388624 | tf_op jit(solution)/shard_map/all_gather | solution.py:138
  485.0 10.5 fusion.88
  495.5 47.1 %all-gather.18.cloned.1.call-done = bf16[2048,2048]{1,0:T(8,128)(2,1)} async-done(((bf16[2048,256]{1,0:T(8,128)(2,1)}), bf16[2048,2048]{1,0:T(8,128)(2,1)}) %all-gather.18.cloned.1.call-update) | async-done | bytes 8388624 | tf_op jit(solution)/shard_map/all_gather | solution.py:139
  542.6 15.3 multiply_convert_fusion.1
  557.9 8.4 fusion.89
  566.4 6.1 convolution_add_fusion
  572.6 9.9 convolution_convert_fusion
  582.8 144.9 %all-reduce.10.cloned.1.call-done = f32[512,2048]{1,0:T(8,128)} async-done(((f32[512,2048]{1,0:T(8,128)}), f32[512,2048]{1,0:T(8,128)}) %all-reduce.10.cloned.1.call-update) | async-done | bytes 4194320 | tf_op jit(solution)/shard_map/psum | solution.py:194
  727.7 4.5 multiply_reduce_fusion
  732.2 83.0 %all-reduce.8.cloned.1.call-done = bf16[512,2048]{1,0:T(8,128)(2,1)} async-done(((bf16[512,2048]{1,0:T(8,128)(2,1)}), bf16[512,2048]{1,0:T(8,128)(2,1)}) %all-reduce.8.cloned.1.call-update) | async-done | bytes 2097168 | tf_op jit(solution)/shard_map/psum | solution.py:189
  815.2 8.1 bitcast_add_fusion
  826.6 20.5 %while.27 = (s32[]{:T(128)}, f32[2,4,512,64]{2,3,1,0:T(8,128)}, f32[2,1024,64]{1,2,0:T(8,128)S(1)}, f32[2,1024,64]{1,2,0:T(8,128)}, pred[512,1024]{1,0:T(8,128)(...) while((s32[]{:T(128)}, f32[2,4,512,64]{2,3,1,0:T(8,128)}, ...), condition=%wide.region_12.13_spmd, body=%wide.region_10.12_spmd.sunk | while | flops 1365768192 | bytes 50255028 | solution.py:112
  828.0 3.3 multiply_convert_fusion.7
  833.8 3.1 fusion.170
  838.3 3.3 multiply_convert_fusion.7
  844.0 3.1 fusion.170
  857.8 3.5 fusion.92
  863.2 5.7 fusion.73
  869.0 3.3 fusion.69
  873.9 9.7 fusion.93
  883.7 9.9 fusion.94
  895.2 10.4 fusion.82
  907.5 105.3 %all-reduce.12.cloned.1.call-done = f32[512,2048]{1,0:T(8,128)} async-done(((f32[512,2048]{1,0:T(8,128)}), f32[512,2048]{1,0:T(8,128)}) %all-reduce.12.cloned.1.call-update) | async-done | bytes 4194320 | tf_op jit(solution)/shard_map/psum | solution.py:220
  1012.7 4.5 fusion.61
  1017.3 24.1 %all-reduce.3 = (f32[2048]{0:T(1024)S(1)}, f32[2048]{0:T(1024)S(1)}) all-reduce(f32[2048]{0:T(1024)S(1)} %get-tuple-element.169, f32[2048]{0:T(1024)S(1)} %get-tuple-element.167), channel_id=10, replica_groups=mesh['fsdp'=4,'ctx'=2,'tp'=4] {'fsdp','ctx'}, use_global_device_ids=true, to_apply=%region_23.24.clone | all-reduce | flops 4096 | bytes 32768
  1042.6 7.8 fusion.58
  1051.4 39.8 %reduce-scatter.10.cloned.1.call-done = f32[256,128]{1,0:T(8,128)} async-done(((f32[2048,128]{1,0:T(8,128)}), f32[256,128]{1,0:T(8,128)}) %reduce-scatter.10.cloned.1.call-update) | async-done | bytes 131088 | tf_op jit(solution)/shard_map/reduce_scatter | solution.py:225
  1091.1 54.9 %reduce-scatter.14.cloned.1.call-done = f32[512,256]{1,0:T(8,128)} async-done(((f32[512,2048]{1,0:T(8,128)}), f32[512,256]{1,0:T(8,128)}) %reduce-scatter.14.cloned.1.call-update) | async-done | bytes 524304 | tf_op jit(solution)/shard_map/reduce_scatter | solution.py:227
  1146.0 55.1 %reduce-scatter.8.cloned.1.call-done = f32[256,512]{1,0:T(8,128)} async-done(((f32[2048,512]{1,0:T(8,128)}), f32[256,512]{1,0:T(8,128)}) %reduce-scatter.8.cloned.1.call-update) | async-done | bytes 524304 | tf_op jit(solution)/shard_map/reduce_scatter | solution.py:224
  1201.1 120.2 %reduce-scatter.16.cloned.1.call-done = f32[256,2048]{1,0:T(8,128)} async-done(((f32[2048,2048]{1,0:T(8,128)}), f32[256,2048]{1,0:T(8,128)}) %reduce-scatter.16.cloned.1.call-update) | async-done | bytes 2097168 | tf_op jit(solution)/shard_map/reduce_scatter | solution.py:228
  1321.3 120.2 %reduce-scatter.18.cloned.1.call-done = f32[256,2048]{1,0:T(8,128)} async-done(((f32[2048,2048]{1,0:T(8,128)}), f32[256,2048]{1,0:T(8,128)}) %reduce-scatter.18.cloned.1.call-update) | async-done | bytes 2097168 | tf_op jit(solution)/shard_map/reduce_scatter | solution.py:229
  1441.6 120.0 %reduce-scatter.20.cloned.1.call-done = f32[2048,256]{1,0:T(8,128)} async-done(((f32[2048,2048]{1,0:T(8,128)}), f32[2048,256]{1,0:T(8,128)}) %reduce-scatter.20.cloned.1.call-update) | async-done | bytes 2097168 | tf_op jit(solution)/shard_map/reduce_scatter | solution.py:230
  (174 shorter events, 64.6 us)
Async XLA Ops:
  7.2 52.0 %all-gather.10.cloned.1.call-start = ((), (), s32[]{:S(2)}) async-start(), calls=%async_computation.7 | async-start | bytes 2359296 | tf_op jit(solution)/shard_map/all_gather | solution.py:133
  7.9 75.0 %all-gather.12.cloned.1.call-start = ((), (), s32[]{:S(2)}) async-start(), calls=%async_computation.8 | async-start | bytes 2359296 | tf_op jit(solution)/shard_map/all_gather | solution.py:136
  19.0 29.3 %copy-start.20 = (f32[8,1,256]{2,1,0:T(1,128)}, f32[8,1,256]{2,1,0:T(1,128)S(1)}, u32[]{:S(2)}) copy-start(f32[8,1,256]{2,1,0:T(1,128)S(1)} %convert_element_type.149) | copy-start | bytes 24580
  29.7 4.8 copy-start.7
  29.9 4.6 copy-start
  33.5 14.8 copy-start.23
  34.5 31.5 %copy-start.13 = (f32[512,32]{0,1:T(8,128)}, f32[512,32]{0,1:T(8,128)S(1)}, u32[]{:S(2)}) copy-start(f32[512,32]{0,1:T(8,128)S(1)} %get-tuple-element.234) | copy-start | bytes 196612
  34.5 4.9 copy-start.22
  34.9 28.2 %copy-start.2 = (bf16[1,512,2048]{2,1,0:T(8,128)(2,1)}, bf16[1,512,2048]{2,1,0:T(8,128)(2,1)S(1)}, u32[]{:S(2)}) copy-start(bf16[1,512,2048]{2,1,0:T(8,128)(2,1)S(1)} %multiply_convert_fusion.5) | copy-start | bytes 6291460
  36.5 18.2 %collective-permute-start = (bf16[512,128]{0,1:T(8,128)(2,1)}, bf16[512,128]{0,1:T(8,128)(2,1)}, u32[]{:S(2)}, u32[]{:S(2)}) collective-permute-start(bf16[512,128]{0,1:T(8,128)(2,1)} %bitcast.31), channel_id=1, source_target_pairs={{0,4},{1,5},{2,6},{3,7},{8,12},{9,13},{10,14},{11,15},{16,20},{17,... | collective-permute-start | bytes 393224 | tf_op jit(solution)/shard_map/ppermute | solution.py:15
  48.3 3.1 copy-start.9
  51.5 4.2 collective-permute-start.1
  54.4 320.4 %all-gather.20.cloned.1.call-start = ((), (), s32[]{:S(2)}) async-start(), calls=%async_computation.22 | async-start | bytes 20971520 | tf_op jit(solution)/shard_map/all_gather | solution.py:181
  67.9 2.4 copy-start.18
  74.2 2.4 copy-start.18
  87.8 1.8 copy-start.27
  87.9 341.1 %all-gather.14.cloned.1.call-start = ((), (), s32[]{:S(2)}) async-start(), calls=%async_computation.9 | async-start | bytes 9437184 | tf_op jit(solution)/shard_map/all_gather | solution.py:137
  88.4 396.6 %all-gather.16.cloned.1.call-start = ((), (), s32[]{:S(2)}) async-start(), calls=%async_computation.10 | async-start | bytes 9437184 | tf_op jit(solution)/shard_map/all_gather | solution.py:138
  89.0 453.6 %all-gather.18.cloned.1.call-start = ((), (), s32[]{:S(2)}) async-start(), calls=%async_computation.11 | async-start | bytes 9437184 | tf_op jit(solution)/shard_map/all_gather | solution.py:139
  89.6 638.1 %all-reduce.10.cloned.1.call-start = ((), (), s32[]{:S(2)}) async-start(), calls=%async_computation.13 | async-start | bytes 8388608 | tf_op jit(solution)/shard_map/psum | solution.py:194
  389.0 2.0 copy-start.1
  557.9 8.4 copy-start.30
  557.9 8.4 copy-start.26
  572.5 242.6 %all-reduce.8.cloned.1.call-start = ((), (), s32[]{:S(2)}) async-start(), calls=%async_computation.12 | async-start | bytes 4194304 | tf_op jit(solution)/shard_map/psum | solution.py:189
  582.5 430.2 %all-reduce.12.cloned.1.call-start = ((), (), s32[]{:S(2)}) async-start(), calls=%async_computation.14 | async-start | bytes 8388608 | tf_op jit(solution)/shard_map/psum | solution.py:220
  815.2 10.1 copy-start.12
  823.3 2.0 copy-start.4
  823.3 3.3 copy-start.19
  826.6 24.6 %copy-start.14 = (f32[512,32]{0,1:T(8,128)S(1)}, f32[512,32]{0,1:T(8,128)}, u32[]{:S(2)}) copy-start(f32[512,32]{0,1:T(8,128)} %copy-done.13) | copy-start | bytes 196612
  826.6 24.6 %copy-start.17 = (f32[512,32]{0,1:T(8,128)S(1)}, f32[512,32]{0,1:T(8,128)}, u32[]{:S(2)}) copy-start(f32[512,32]{0,1:T(8,128)} %get-tuple-element.232) | copy-start | bytes 196612
  828.0 3.3 copy-start.15
  838.3 3.3 copy-start.15
  847.1 5.5 copy-start.6
  848.3 6.5 collective-permute-start.3
  849.7 4.3 collective-permute-start.2
  857.8 3.6 copy-start.3
  857.8 193.6 %reduce-scatter.12.cloned.1.call-start = ((), (), s32[]{:S(2)}) async-start(), calls=%async_computation.17 | async-start | bytes 1179648 | tf_op jit(solution)/shard_map/reduce_scatter | solution.py:226
  861.4 229.8 %reduce-scatter.10.cloned.1.call-start = ((), (), s32[]{:S(2)}) async-start(), calls=%async_computation.16 | async-start | bytes 1179648 | tf_op jit(solution)/shard_map/reduce_scatter | solution.py:225
  863.2 282.8 %reduce-scatter.14.cloned.1.call-start = ((), (), s32[]{:S(2)}) async-start(), calls=%async_computation.18 | async-start | bytes 4718592 | tf_op jit(solution)/shard_map/reduce_scatter | solution.py:227
  868.9 332.2 %reduce-scatter.8.cloned.1.call-start = ((), (), s32[]{:S(2)}) async-start(), calls=%async_computation.15 | async-start | bytes 4718592 | tf_op jit(solution)/shard_map/reduce_scatter | solution.py:224
  872.3 1.6 copy-start.11
  872.3 449.0 %reduce-scatter.16.cloned.1.call-start = ((), (), s32[]{:S(2)}) async-start(), calls=%async_computation.19 | async-start | bytes 18874368 | tf_op jit(solution)/shard_map/reduce_scatter | solution.py:228
  883.7 557.9 %reduce-scatter.18.cloned.1.call-start = ((), (), s32[]{:S(2)}) async-start(), calls=%async_computation.20 | async-start | bytes 18874368 | tf_op jit(solution)/shard_map/reduce_scatter | solution.py:229
  893.6 1.6 copy-start.29
  893.6 668.0 %reduce-scatter.20.cloned.1.call-start = ((), (), s32[]{:S(2)}) async-start(), calls=%async_computation.21 | async-start | bytes 18874368 | tf_op jit(solution)/shard_map/reduce_scatter | solution.py:230
  905.6 107.2 %copy-start.21 = (f32[8,1,256]{2,1,0:T(1,128)S(1)}, f32[8,1,256]{2,1,0:T(1,128)}, u32[]{:S(2)}) copy-start(f32[8,1,256]{2,1,0:T(1,128)} %copy-done.20) | copy-start | bytes 24580
  905.6 107.2 %copy-start.24 = (f32[512]{0:T(512)S(1)}, f32[512]{0:T(512)}, u32[]{:S(2)}) copy-start(f32[512]{0:T(512)} %copy-done.23) | copy-start | bytes 6148
  907.5 135.2 %copy-start.25 = (f32[512]{0:T(512)S(1)}, f32[512]{0:T(512)}, u32[]{:S(2)}) copy-start(f32[512]{0:T(512)} %get-tuple-element.235) | copy-start | bytes 6148
  (6 other events, 6.5 us)
Sparse Core Ops, SparseCore 0:
  9.9 31.1 all-gather.9
  54.5 28.3 all-gather.11
  88.0 286.7 all-gather.19
  376.5 52.4 all-gather.13
  430.7 54.2 all-gather.15
  486.7 55.8 all-gather.17
  572.6 154.9 all-reduce.9
  730.0 85.0 all-reduce.7
  857.9 154.7 all-reduce.11
  1016.3 34.9 reduce-scatter.11
  1055.1 35.9 reduce-scatter.9
  1094.9 51.0 reduce-scatter.13
  1149.9 51.1 reduce-scatter.7
  1205.1 116.1 reduce-scatter.15
  1325.3 116.1 reduce-scatter.17
  1445.5 115.9 reduce-scatter.19
